TPU v7x, 32 devices: a whole 2x2x4 slice. The times are simulated.
32 devices in a mesh: groups: 2 (over x), req: 8 (over z, core), row: 2 (over y).
Axes of the slice: x: 2, y: 2, z: 4, core: 2. Of those that a mesh axis runs over, the one named last changes fastest.
Arguments:
- latents: bfloat16 [16, 2, 4, 2560], P('groups', None, 'row', 'req'), parts along dimension 0, may hold values from -8 to 8
- dispatch_plan: int32 [16], P('groups'), parts along dimension 0, may hold values from 0 to 7, each once
- span_counts: int32 [8], P('groups'), parts along dimension 0, may hold values from 1 to 4, 8 in all
- in_weight: bfloat16 [432, 384], replicated, may hold values from -0.3125 to 0.3125
- in_bias: float32 [384], replicated, may hold values from -3 to 3
- norm_gain: float32 [384], replicated, may hold values from 0.5 to 1.5
- norm_bias: float32 [384], replicated, may hold values from -3 to 3
- mid_weight: bfloat16 [27, 384, 384], replicated, may hold values from -0.0625 to 0.0625
- mid_bias: float32 [384], replicated, may hold values from -3 to 3
Outputs:
- decoded: bfloat16 [16, 2, 4, 61440], P(('groups', 'req'), None, 'row'), parts along dimension 0
There are 2 independent parts, one for each index of `groups`. A program takes and returns all parts, laid end to end along the dimension named above; an argument that names none is the same for every part. Nothing has to cross between parts.
Inputs may be any that keep to these rules, and one draw needn't show every extreme that they name: `span_counts`: the counts sum to 8.
All inputs are finite; a program needn't handle non-finite values.
Results may differ from a plain program's by a relative error of at most 0.0029.
Values may be sent and summed in bfloat16 or wider, within the bound.
A program may use at most 64 MiB of HBM per device.

v0:
```python
import functools

import jax
import jax.numpy as jnp
from jax import lax
from jax.experimental import pallas as pl
from jax.experimental.pallas import tpu as pltpu
from jax.sharding import PartitionSpec as P

C_LAT = 16
G = 32
CF = 2
W = 160
LANES = 128
DEPTH = 3
MESH = pl.DeviceIdType.MESH


def span_kernel(
    req_n,
    row_n,
    lat_hbm,
    plan_hbm,
    counts_hbm,
    in_w_hbm,
    in_b_hbm,
    gain_hbm,
    nbias_hbm,
    mid_w_hbm,
    mid_b_hbm,
    out_ref,
    lat_ref,
    plan_ref,
    counts_ref,
    in_w_ref,
    in_b_ref,
    gain_ref,
    nbias_ref,
    mid_b_ref,
    sel,
    x_ref,
    mid_w,
    in_w,
    pair_rows,
    pair_time,
    hid,
    act,
    lines,
    fanned,
    sems,
    send_sems,
    recv_sems,
):
    me = lax.axis_index("req")
    me_row = lax.axis_index("row")
    devices = req_n * row_n
    flat = me_row * req_n + me
    rows_here = lat_ref.shape[2]
    row0 = me_row * rows_here

    def peer(k):
        target = lax.rem(flat + k, devices)
        return {"row": target // req_n, "req": lax.rem(target, req_n)}

    barrier = pltpu.get_barrier_semaphore()
    for k in range(1, devices):
        pl.semaphore_signal(barrier, inc=1, device_id=peer(k), device_id_type=MESH)
    loads = [
        pltpu.make_async_copy(source, target, sems.at[9 + n])
        for n, (source, target) in enumerate(
            (
                (plan_hbm, plan_ref),
                (lat_hbm, lat_ref),
                (counts_hbm, counts_ref),
                (in_w_hbm, in_w_ref),
                (in_b_hbm, in_b_ref),
                (gain_hbm, gain_ref),
                (nbias_hbm, nbias_ref),
                (mid_b_hbm, mid_b_ref),
            )
        )
    ]
    for load in loads:
        load.start()
    copies = []
    for tap in range(9):
        copy = pltpu.make_async_copy(
            mid_w_hbm.at[pl.ds(3 * tap, 3)], mid_w.at[pl.ds(3 * tap, 3)], sems.at[tap]
        )
        copy.start()
        copies.append(copy)
    loads[0].wait()
    loads[1].wait()
    for d in range(DEPTH - 1):
        sel[d] = jnp.zeros_like(sel[d])
    for d in range(req_n):
        span = lat_ref[plan_ref[d]].astype(jnp.float32)
        sel[d + DEPTH - 1] = jnp.concatenate([span[f] for f in range(CF)], axis=1).astype(sel.dtype)
    pl.semaphore_wait(barrier, devices - 1)
    sends = []
    for k in range(1, devices):
        where = peer(k)
        send = pltpu.make_async_remote_copy(
            src_ref=sel.at[pl.ds(where["req"], DEPTH)],
            dst_ref=x_ref.at[me_row, me],
            send_sem=send_sems.at[k],
            recv_sem=recv_sems.at[k],
            device_id=where,
            device_id_type=MESH,
        )
        send.start()
        sends.append(send)
    x_ref[me_row, me] = sel[pl.ds(me, DEPTH)]
    for load in loads[2:]:
        load.wait()

    frames_in = DEPTH * CF
    height = row_n * rows_here
    lanes = x_ref.shape[4] // CF
    width = req_n * lanes // C_LAT
    blocks = width * C_LAT // LANES
    chans = in_w_ref.shape[1]
    outs = frames_in - 2
    in_b = in_b_ref[...].reshape(1, chans)
    gain = gain_ref[...].reshape(1, chans)
    nbias = nbias_ref[...].reshape(1, chans)
    mid_b = mid_b_ref[...].reshape(1, chans)
    def keep_of(d):
        start = jnp.int32(0)
        first = d <= 0
        for r in range(counts_ref.shape[0]):
            first = jnp.logical_or(first, start == d)
            start = start + counts_ref[r]
        return jnp.where(first, 0.0, 1.0).astype(jnp.float32)

    keep_own = keep_of(me)
    keep_prev = keep_of(me - 1)

    half = LANES // 2
    three = 3 * C_LAT
    in_w[...] = jnp.zeros_like(in_w)
    for t in range(3):
        for i in range(3):
            if i < 2:
                base = t * LANES + i * half
            else:
                base = 3 * LANES + t * half
            in_w[base : base + three, :] = in_w_ref[(3 * t + i) * three : (3 * t + i + 1) * three, :]

    zero_slab = jnp.zeros((width, LANES), jnp.bfloat16)
    for f in range(frames_in):
        pair_rows[f, 0] = zero_slab
    for f in range(frames_in + 1):
        pair_time[f, height] = zero_slab
    for y in range(height):
        pair_time[frames_in, y] = zero_slab

    lane = lax.broadcasted_iota(jnp.int32, (blocks, LANES), 1)
    low = lane < C_LAT
    high = jnp.logical_and(lane >= 2 * C_LAT, lane < three)
    left = lane < half
    nothing = jnp.zeros((1, LANES), jnp.float32)

    def place_row(f, y, here):
        cells = lines[pl.ds(here, blocks, stride=rows_here), :]
        turned = [pltpu.roll(cells, (C_LAT - C_LAT * p) % LANES, 1) if p != 1 else cells for p in range(8)]
        for p in range(8):
            window = turned[p]
            other = turned[(p + 4) % 8]
            if p == 0:
                before = jnp.concatenate([nothing, window[:-1]], axis=0)
                window = jnp.where(low, before, window)
                other = pltpu.roll(window, half, 1)
            if p == 7:
                after = jnp.concatenate([window[1:], nothing], axis=0)
                window = jnp.where(high, after, window)
                other = pltpu.roll(window, half, 1)
            fanned[here, pl.ds(p, blocks, stride=8), :] = jnp.where(left, window, other)
        both = fanned[here].astype(jnp.bfloat16)
        pair_rows[f, y + 1, :, :half] = both[:, :half]
        pair_rows[f, y, :, half:] = both[:, half:]
        pair_time[f + 1, y, :, :half] = both[:, :half]
        pair_time[f, y, :, half:] = both[:, half:]

    for send in sends:
        send.wait()

    @pl.loop(0, DEPTH)
    def _(span):
        keep = jnp.where(span == 0, keep_prev, jnp.where(span == 1, keep_own, 1.0))

        @pl.loop(0, row_n)
        def _(r):
            shards = [x_ref[r, q, span].astype(jnp.float32) * keep for q in range(req_n)]
            for frame in range(CF):
                merged = jnp.concatenate(
                    [shard[:, frame * lanes : (frame + 1) * lanes] for shard in shards], axis=1
                )
                for b in range(blocks):
                    lines[b * rows_here : (b + 1) * rows_here, :] = merged[:, b * LANES : (b + 1) * LANES]
                for here in range(rows_here):
                    place_row(span * CF + frame, r * rows_here + here, here)

    sums = []
    cells = height * width
    for f in range(outs):
        taps = [
            pair_rows[f, :height],
            pair_rows[f + 1, :height],
            pair_rows[f + 2, :height],
            pair_time[f + 1, 1:],
            pair_time[f + 3, 1:],
        ]
        stacked = jnp.concatenate([tap.reshape(cells, LANES) for tap in taps], axis=1)
        hidden = jnp.dot(stacked, in_w[...], preferred_element_type=jnp.float32) + in_b
        hid[f] = hidden.reshape(height, width, chans)
        sums.append(jnp.sum(hidden, axis=0, keepdims=True))
        sums.append(jnp.sum(hidden * hidden, axis=0, keepdims=True))
    per_group = chans // G
    down = lax.broadcasted_iota(jnp.int32, (chans, chans), 0) // per_group
    over = lax.broadcasted_iota(jnp.int32, (chans, chans), 1) // per_group
    same = jnp.where(down == over, 1.0, 0.0).astype(jnp.float32)
    grouped = jnp.dot(
        jnp.concatenate(sums, axis=0),
        same,
        precision=lax.Precision.HIGHEST,
        preferred_element_type=jnp.float32,
    ) / (cells * per_group)

    span_rows = rows_here + 2
    for f in range(outs):
        mean = grouped[2 * f : 2 * f + 1]
        var = grouped[2 * f + 1 : 2 * f + 2] - mean * mean
        scale = lax.rsqrt(var + 1e-06) * gain

        @pl.loop(0, span_rows)
        def _(y, f=f, mean=mean, scale=scale):
            row = row0 + y - 1
            inside = jnp.logical_and(row >= 0, row < height)
            @pl.when(inside)
            def _():
                value = (hid[f, row] - mean) * scale + nbias
                value = 0.5 * value * (1.0 + jnp.tanh(0.5 * value))
                if f < CF:
                    value = value * keep_own
                act[f, y] = value.astype(jnp.bfloat16)

            @pl.when(jnp.logical_not(inside))
            def _():
                act[f, y] = jnp.zeros((width, chans), jnp.bfloat16)

    many = CF * rows_here * width
    for copy in copies:
        copy.wait()
    slabs = []
    weights = []
    for t in range(3):
        for i in range(3):
            tap = 3 * (3 * t + i)
            slabs.append(act[t : t + CF, i : i + rows_here].reshape(many, chans))
            weights.append(jnp.concatenate([mid_w[tap + j] for j in range(3)], axis=1))
    columns = jnp.dot(
        jnp.concatenate(slabs, axis=1),
        jnp.concatenate(weights, axis=0),
        preferred_element_type=jnp.float32,
    ).reshape(CF * rows_here, width, 3 * chans)
    nil = jnp.zeros((1, chans), jnp.float32)
    for f in range(CF):
        for y in range(rows_here):
            part = columns[f * rows_here + y]
            total = hid[outs - CF + f, row0 + y] + mid_b + part[:, chans : 2 * chans]
            total = total + jnp.concatenate([nil, part[:-1, :chans]], axis=0)
            total = total + jnp.concatenate([part[1:, 2 * chans :], nil], axis=0)
            out_ref[f, y] = total.astype(jnp.bfloat16)


def spans(latents, dispatch_plan, span_counts, in_weight, in_bias, norm_gain, norm_bias, mid_weight, mid_bias):
    req_n = lax.axis_size("req")
    row_n = lax.axis_size("row")
    frames, rows_here, lanes = latents.shape[1:]
    chans = in_weight.shape[1]
    frames_in = DEPTH * CF
    outs = frames_in - 2
    height = row_n * rows_here
    blocks = W * C_LAT // LANES
    grant = mid_weight.size * 2 + 4 * chans * W * (outs * height + CF * rows_here)
    grant += 2 * chans * W * outs * (rows_here + 2) + 4 * (frames_in + 1) * (height + 1) * W * LANES
    grant += (8 << 20)
    return pl.pallas_call(
        functools.partial(span_kernel, req_n, row_n),
        out_shape=jax.ShapeDtypeStruct((CF, rows_here, W, chans), jnp.bfloat16),
        in_specs=[pl.BlockSpec(memory_space=pltpu.HBM)] * 9,
        out_specs=pl.BlockSpec(memory_space=pltpu.VMEM),
        scratch_shapes=[
            pltpu.VMEM(latents.shape, latents.dtype),
            pltpu.SMEM(dispatch_plan.shape, jnp.int32),
            pltpu.SMEM(span_counts.shape, jnp.int32),
            pltpu.VMEM(in_weight.shape, in_weight.dtype),
            pltpu.VMEM((chans,), jnp.float32),
            pltpu.VMEM((chans,), jnp.float32),
            pltpu.VMEM((chans,), jnp.float32),
            pltpu.VMEM((chans,), jnp.float32),
            pltpu.VMEM((req_n + DEPTH - 1, rows_here, frames * lanes), latents.dtype),
            pltpu.VMEM((row_n, req_n, DEPTH, rows_here, frames * lanes), latents.dtype),
            pltpu.VMEM(mid_weight.shape, jnp.bfloat16),
            pltpu.VMEM((5 * LANES, chans), jnp.bfloat16),
            pltpu.VMEM((frames_in, height + 1, W, LANES), jnp.bfloat16),
            pltpu.VMEM((frames_in + 1, height + 1, W, LANES), jnp.bfloat16),
            pltpu.VMEM((outs, height, W, chans), jnp.float32),
            pltpu.VMEM((outs, rows_here + 2, W, chans), jnp.bfloat16),
            pltpu.VMEM((blocks * rows_here, LANES), jnp.float32),
            pltpu.VMEM((rows_here, W, LANES), jnp.float32),
            pltpu.SemaphoreType.DMA((17,)),
            pltpu.SemaphoreType.DMA((req_n * row_n,)),
            pltpu.SemaphoreType.DMA((req_n * row_n,)),
        ],
        compiler_params=pltpu.CompilerParams(
            collective_id=0, has_side_effects=True, vmem_limit_bytes=grant
        ),
        name="spans",
    )(
        *(
            pltpu.with_memory_space_constraint(arg, pltpu.HBM)
            for arg in (
                latents,
                dispatch_plan,
                span_counts,
                in_weight,
                in_bias,
                norm_gain,
                norm_bias,
                mid_weight,
                mid_bias,
            )
        )
    )


def local(
    latents,
    dispatch_plan,
    span_counts,
    in_weight,
    in_bias,
    norm_gain,
    norm_bias,
    mid_weight,
    mid_bias,
):
    rows_here = latents.shape[2]
    chans = mid_weight.shape[2]
    mixed = spans(
        latents,
        dispatch_plan,
        span_counts,
        in_weight,
        in_bias,
        norm_gain,
        norm_bias,
        mid_weight,
        mid_bias,
    )
    return mixed.reshape(1, CF, rows_here, W * chans)


def solution(mesh):
    placed = (
        P("groups", None, "row", "req"),
        P("groups"),
        P("groups"),
        P(),
        P(),
        P(),
        P(),
        P(),
        P(),
    )
    return jax.shard_map(
        local,
        mesh=mesh,
        in_specs=placed,
        out_specs=P(("groups", "req"), None, "row", None),
        check_vma=False,
    )
```

profile of v0, /device:TPU:0, one launch (start us, length us, event | category | flops | bytes accessed | tf_op | source)
XLA Modules:
  0.0 24.7 jit_solution(13976639268714299152)
XLA Ops:
  0.0 23.8 %spans.1 = bf16[2,2,160,384]{3,2,1,0:T(8,128)(2,1)S(1)} custom-call(bf16[8,2,2,320]{3,2,1,0:T(2,128)(2,1)} %lat_hbm.1, s32[8]{0:T(128)} %plan_hbm.1, s32[4]{0:T(128)} %counts_hbm.1, bf16[432,384]{1,0:T(8,128)(2,1)} %in_w_hbm.1, f32[384]{0:T(512)} %in_b_hbm.1, f32[384]{0:T(512)} %gain_hbm.1, f32[384]{0:T(512)} %nbias_hbm.1, bf16[27,384,384]{2,1,0:T(8,128)(2,1)} %mid_w_hbm.1, ...), custom_call_target="tpu_custom_call" | custom-call | tf_op jit(solution)/shard_map/spans/pallas_call | solution.py:289
  23.8 0.9 %reshape.3 = bf16[1,2,2,61440]{3,2,1,0:T(2,128)(2,1)} reshape(bf16[2,2,160,384]{3,2,1,0:T(8,128)(2,1)S(1)} %spans.1) | data formatting | bytes 983040 | tf_op jit(solution)/shard_map/reshape | solution.py:363
where the time goes:
time: 24.9 us; the launch traced here: 24.7 us
  Pallas kernels  23.8 us (96%)
  local copies, waits for them, and re-layouts  0.86 us (3%)
    pallas_call x1, Pallas kernels, spans(): pl.pallas_call(functools.partial(span_kernel, req_n, row_n), out_shape=ja...  23.8 us
    reshape x1, local copies, waits for them, and re-layouts, local(): return mixed.reshape(1, CF, rows_here, W * chans)  0.86 us

commit v1 on v0

--- a/solution.py
+++ b/solution.py
@@ -336,6 +336,367 @@
     )
 
 
+def edge_kernel(
+    req_n,
+    lat_hbm,
+    plan_hbm,
+    counts_hbm,
+    in_w_hbm,
+    in_b_hbm,
+    gain_hbm,
+    nbias_hbm,
+    mid_w_hbm,
+    mid_b_hbm,
+    out_ref,
+    lat_ref,
+    plan_ref,
+    counts_ref,
+    in_w_ref,
+    in_b_ref,
+    gain_ref,
+    nbias_ref,
+    mid_b_ref,
+    sel,
+    x_ref,
+    mid_w,
+    in_w,
+    same_ref,
+    slab,
+    tail,
+    hid,
+    act,
+    lines,
+    fan,
+    sems,
+    send_sems,
+    recv_sems,
+):
+    me = lax.axis_index("req")
+    me_row = lax.axis_index("row")
+    row_n = 2
+    devices = req_n * row_n
+    flat = me_row * req_n + me
+    rows_here = lat_ref.shape[2]
+
+    def peer(k):
+        target = lax.rem(flat + k, devices)
+        return {"row": target // req_n, "req": lax.rem(target, req_n)}
+
+    def turned(i):
+        return jnp.where(me_row == 0, i, 2 - i)
+
+    barrier = pltpu.get_barrier_semaphore()
+    for k in range(1, devices):
+        pl.semaphore_signal(barrier, inc=1, device_id=peer(k), device_id_type=MESH)
+    loads = [
+        pltpu.make_async_copy(source, target, sems.at[n])
+        for n, (source, target) in enumerate(
+            (
+                (plan_hbm, plan_ref),
+                (lat_hbm, lat_ref),
+                (counts_hbm, counts_ref),
+                (in_b_hbm, in_b_ref),
+                (gain_hbm, gain_ref),
+                (nbias_hbm, nbias_ref),
+                (mid_b_hbm, mid_b_ref),
+            )
+        )
+    ]
+    three = 3 * C_LAT
+    in_copies = []
+    copies = []
+    for t in range(3):
+        for i in range(3):
+            n = 3 * t + i
+            start = pl.multiple_of((3 * t + turned(i)) * three, C_LAT)
+            in_copies.append(
+                pltpu.make_async_copy(
+                    in_w_hbm.at[pl.ds(start, three)], in_w_ref.at[pl.ds(n * three, three)], sems.at[7 + n]
+                )
+            )
+            copies.append(
+                pltpu.make_async_copy(
+                    mid_w_hbm.at[pl.ds(3 * (3 * t + turned(i)), 3)], mid_w.at[pl.ds(3 * n, 3)], sems.at[16 + n]
+                )
+            )
+    for copy in loads + in_copies + copies:
+        copy.start()
+    loads[0].wait()
+    loads[1].wait()
+    for flip in range(2):
+        for d in range(DEPTH - 1):
+            sel[flip, d] = jnp.zeros_like(sel[flip, d])
+    for d in range(req_n):
+        span = lat_ref[plan_ref[d]].astype(jnp.float32)
+        both = jnp.concatenate([span[f] for f in range(CF)], axis=1)
+        sel[0, d + DEPTH - 1] = both.astype(sel.dtype)
+        sel[1, d + DEPTH - 1] = jnp.concatenate([both[1:], both[:1]], axis=0).astype(sel.dtype)
+    pl.semaphore_wait(barrier, devices - 1)
+    early = DEPTH - 1
+    sends = [[], []]
+    for part, (base, count) in enumerate(((0, early), (early, 1))):
+        for k in range(1, devices):
+            where = peer(k)
+            there = where["row"]
+            send = pltpu.make_async_remote_copy(
+                src_ref=sel.at[there, pl.ds(where["req"] + base, count)],
+                dst_ref=x_ref.at[lax.rem(me_row + there, 2), me, pl.ds(base, count)],
+                send_sem=send_sems.at[part, k],
+                recv_sem=recv_sems.at[part, k],
+                device_id=where,
+                device_id_type=MESH,
+            )
+            send.start()
+            sends[part].append(send)
+    x_ref[0, me] = sel[me_row, pl.ds(me, DEPTH)]
+    for copy in loads[2:] + in_copies:
+        copy.wait()
+
+    frames_in = DEPTH * CF
+    height = row_n * rows_here
+    lanes = x_ref.shape[4] // CF
+    width = req_n * lanes // C_LAT
+    blocks = width * C_LAT // LANES
+    chans = in_w_ref.shape[1]
+    outs = frames_in - 2
+    in_b = in_b_ref[...].reshape(1, chans)
+    gain = gain_ref[...].reshape(1, chans)
+    nbias = nbias_ref[...].reshape(1, chans)
+    mid_b = mid_b_ref[...].reshape(1, chans)
+
+    def keep_of(d):
+        start = jnp.int32(0)
+        first = d <= 0
+        for r in range(counts_ref.shape[0]):
+            first = jnp.logical_or(first, start == d)
+            start = start + counts_ref[r]
+        return jnp.where(first, 0.0, 1.0).astype(jnp.float32)
+
+    keep_own = keep_of(me)
+    keep_prev = keep_of(me - 1)
+
+    two = 2 * C_LAT
+    taps_of = (((1, 2, None), (0, 1, 2)), ((2, 0, 1), (1, None, 0)))
+    for g in range(2):
+        for o in range(2):
+            columns = slice(o * chans, (o + 1) * chans)
+            for t in range(3):
+                for n, i in enumerate(taps_of[g][o]):
+                    size = two if n == 2 else three
+                    base = t * LANES + n * three
+                    if i is None:
+                        in_w[g, base : base + size, columns] = jnp.zeros((size, chans), jnp.bfloat16)
+                    else:
+                        tap = (3 * t + i) * three
+                        in_w[g, base : base + size, columns] = in_w_ref[tap : tap + size, :]
+                base = 3 * LANES + t * C_LAT
+                i = taps_of[g][o][2]
+                if i is None:
+                    in_w[g, base : base + C_LAT, columns] = jnp.zeros((C_LAT, chans), jnp.bfloat16)
+                else:
+                    tap = (3 * t + i) * three + two
+                    in_w[g, base : base + C_LAT, columns] = in_w_ref[tap : tap + C_LAT, :]
+        in_w[g, 3 * LANES + three :, :] = jnp.zeros((LANES - three, 2 * chans), jnp.bfloat16)
+    for f in range(outs):
+        tail[f] = jnp.zeros((width, LANES), jnp.bfloat16)
+    per_group = chans // G
+    down = lax.broadcasted_iota(jnp.int32, (chans, chans), 0) // per_group
+    over = lax.broadcasted_iota(jnp.int32, (chans, chans), 1) // per_group
+    same_ref[...] = jnp.where(down == over, 1.0, 0.0).astype(jnp.bfloat16)
+
+    lane = lax.broadcasted_iota(jnp.int32, (blocks, LANES), 1)
+    nothing = jnp.zeros((1, LANES), jnp.float32)
+
+    def window(cells, p, place):
+        view = pltpu.roll(cells, (place + C_LAT - C_LAT * p) % LANES, 1)
+        if p == 0:
+            before = jnp.concatenate([nothing, view[:-1]], axis=0)
+            mine = jnp.logical_and(lane >= place, lane < place + C_LAT)
+            view = jnp.where(mine, before, view)
+        if p == 7:
+            after = jnp.concatenate([view[1:], nothing], axis=0)
+            edge = (place + two) % LANES
+            mine = jnp.logical_and(lane >= edge, lane < edge + C_LAT)
+            view = jnp.where(mine, after, view)
+        return view
+
+    def place_frame(f, slot):
+        cells = [lines[slot, y // 2, pl.ds(y % 2, blocks, stride=2), :] for y in range(4)]
+        for p in range(8):
+            third = window(cells[2], p, 2 * three)
+            inner = jnp.where(lane < 2 * three, window(cells[1], p, three), third)
+            rows = pl.ds(p, blocks, stride=8)
+            fan[slot, 0, rows, :] = jnp.where(lane < three, window(cells[0], p, 0), inner)
+            fan[slot, 1, rows, :] = jnp.where(lane < three, window(cells[3], p, 0), inner)
+            fan[slot, 2, rows, :] = third
+        for g in range(2):
+            slab[g, f] = fan[slot, g].astype(jnp.bfloat16)
+        last = fan[slot, 2]
+        for t in range(3):
+            if 0 <= f - t < outs:
+                at = slice(t * C_LAT, (t + 1) * C_LAT)
+                moved = pltpu.roll(last, t * C_LAT, 1) if t else last
+                tail[f - t, :, at] = moved[:, at].astype(jnp.bfloat16)
+
+    def place_span(span, keep):
+        for r in range(2):
+            shards = []
+            for q in range(req_n):
+                shard = x_ref[r, q, span].astype(jnp.float32)
+                shards.append(shard if keep is None else shard * keep)
+            for frame in range(CF):
+                merged = jnp.concatenate(
+                    [shard[:, frame * lanes : (frame + 1) * lanes] for shard in shards], axis=1
+                )
+                for b in range(blocks):
+                    lines[frame, r, b * 2 : (b + 1) * 2, :] = merged[:, b * LANES : (b + 1) * LANES]
+        for frame in range(CF):
+            place_frame(span * CF + frame, frame)
+
+    def first_conv(f0):
+        sums = []
+        for g in range(2):
+            stacked = jnp.concatenate(
+                [slab[g, f0 + t : f0 + t + 2].reshape(2 * width, LANES) for t in range(3)]
+                + [tail[f0 : f0 + 2].reshape(2 * width, LANES)],
+                axis=1,
+            )
+            both = jnp.dot(stacked, in_w[g], preferred_element_type=jnp.float32)
+            for f in range(2):
+                total = None
+                for o in range(2):
+                    part = both[f * width : (f + 1) * width, o * chans : (o + 1) * chans] + in_b
+                    hid[f0 + f, 2 * g + o] = part
+                    pair = (jnp.sum(part, axis=0, keepdims=True), jnp.sum(part * part, axis=0, keepdims=True))
+                    total = pair if total is None else (total[0] + pair[0], total[1] + pair[1])
+                sums.append(total)
+        rows = []
+        for f in range(2):
+            rows.append(sums[f][0] + sums[2 + f][0])
+            rows.append(sums[f][1] + sums[2 + f][1])
+        rows = jnp.concatenate(rows, axis=0)
+        upper = rows.astype(jnp.bfloat16)
+        rest = rows - upper.astype(jnp.float32)
+        middle = rest.astype(jnp.bfloat16)
+        lower = (rest - middle.astype(jnp.float32)).astype(jnp.bfloat16)
+        grouped = jnp.dot(
+            jnp.concatenate([upper, middle, lower], axis=0), same_ref[...], preferred_element_type=jnp.float32
+        )
+        grouped = (grouped[0:4] + grouped[4:8] + grouped[8:12]) / (height * width * per_group)
+        for f in range(2):
+            mean = grouped[2 * f : 2 * f + 1]
+            var = grouped[2 * f + 1 : 2 * f + 2] - mean * mean
+            scale = lax.rsqrt(var + 1e-06) * gain
+            half_scale = 0.5 * scale
+            half_shift = 0.5 * (nbias - mean * scale)
+            if f0 + f < CF:
+                half_scale = half_scale * keep_own
+                half_shift = half_shift * keep_own
+            for s in range(3):
+                value = hid[f0 + f, s] * half_scale + half_shift
+                act[f0 + f, s] = (value * (1.0 + jnp.tanh(value))).astype(jnp.bfloat16)
+
+    for send in sends[0]:
+        send.wait()
+    place_span(0, keep_prev)
+    place_span(1, keep_own)
+    first_conv(0)
+    for send in sends[1]:
+        send.wait()
+    place_span(2, None)
+    first_conv(2)
+
+    many = CF * width
+    for copy in copies:
+        copy.wait()
+    nil = jnp.zeros((1, 2 * LANES), jnp.float32)
+    for c0, c1 in ((0, 2 * LANES), (2 * LANES, chans)):
+        for o in (1, 0):
+            slabs = []
+            weights = []
+            for t in range(3):
+                for s in range(3):
+                    i = s - o + 1
+                    if 0 <= i < 3 and s - o < 2:
+                        tap = 3 * (3 * t + i)
+                        slabs.append(act[t : t + CF, s].reshape(many, chans))
+                        weights.append(jnp.concatenate([mid_w[tap + j, :, c0:c1] for j in range(3)], axis=1))
+            columns = jnp.dot(
+                jnp.concatenate(slabs, axis=1),
+                jnp.concatenate(weights, axis=0),
+                preferred_element_type=jnp.float32,
+            )
+            size = c1 - c0
+            where = lax.rem(me_row + o, 2)
+            for f in range(CF):
+                part = columns[f * width : (f + 1) * width]
+                total = hid[outs - CF + f, o, :, c0:c1] + mid_b[:, c0:c1] + part[:, size : 2 * size]
+                total = total + jnp.concatenate([nil[:, :size], part[:-1, :size]], axis=0)
+                total = total + jnp.concatenate([part[1:, 2 * size :], nil[:, :size]], axis=0)
+                out_ref[f, where, :, c0:c1] = total.astype(jnp.bfloat16)
+
+
+def edge_spans(latents, dispatch_plan, span_counts, in_weight, in_bias, norm_gain, norm_bias, mid_weight, mid_bias):
+    req_n = lax.axis_size("req")
+    row_n = lax.axis_size("row")
+    frames, rows_here, lanes = latents.shape[1:]
+    chans = in_weight.shape[1]
+    frames_in = DEPTH * CF
+    outs = frames_in - 2
+    height = row_n * rows_here
+    width = req_n * lanes // C_LAT
+    blocks = width * C_LAT // LANES
+    return pl.pallas_call(
+        functools.partial(edge_kernel, req_n),
+        out_shape=jax.ShapeDtypeStruct((CF, rows_here, width, chans), jnp.bfloat16),
+        in_specs=[pl.BlockSpec(memory_space=pltpu.HBM)] * 9,
+        out_specs=pl.BlockSpec(memory_space=pltpu.VMEM),
+        scratch_shapes=[
+            pltpu.VMEM(latents.shape, latents.dtype),
+            pltpu.SMEM(dispatch_plan.shape, jnp.int32),
+            pltpu.SMEM(span_counts.shape, jnp.int32),
+            pltpu.VMEM(in_weight.shape, in_weight.dtype),
+            pltpu.VMEM((chans,), jnp.float32),
+            pltpu.VMEM((chans,), jnp.float32),
+            pltpu.VMEM((chans,), jnp.float32),
+            pltpu.VMEM((chans,), jnp.float32),
+            pltpu.VMEM((2, req_n + DEPTH - 1, rows_here, frames * lanes), latents.dtype),
+            pltpu.VMEM((row_n, req_n, DEPTH, rows_here, frames * lanes), latents.dtype),
+            pltpu.VMEM(mid_weight.shape, jnp.bfloat16),
+            pltpu.VMEM((2, 4 * LANES, 2 * chans), jnp.bfloat16),
+            pltpu.VMEM((chans, chans), jnp.bfloat16),
+            pltpu.VMEM((2, frames_in, width, LANES), jnp.bfloat16),
+            pltpu.VMEM((outs, width, LANES), jnp.bfloat16),
+            pltpu.VMEM((outs, height, width, chans), jnp.float32),
+            pltpu.VMEM((outs, rows_here + 1, width, chans), jnp.bfloat16),
+            pltpu.VMEM((CF, 2, 2 * blocks, LANES), jnp.float32),
+            pltpu.VMEM((CF, 3, width, LANES), jnp.float32),
+            pltpu.SemaphoreType.DMA((25,)),
+            pltpu.SemaphoreType.DMA((2, req_n * row_n)),
+            pltpu.SemaphoreType.DMA((2, req_n * row_n)),
+        ],
+        compiler_params=pltpu.CompilerParams(
+            collective_id=0, has_side_effects=True, vmem_limit_bytes=48 << 20
+        ),
+        name="edge_spans",
+    )(
+        *(
+            pltpu.with_memory_space_constraint(arg, pltpu.HBM)
+            for arg in (
+                latents,
+                dispatch_plan,
+                span_counts,
+                in_weight,
+                in_bias,
+                norm_gain,
+                norm_bias,
+                mid_weight,
+                mid_bias,
+            )
+        )
+    )
+
+
 def local(
     latents,
     dispatch_plan,
@@ -349,7 +710,8 @@
 ):
     rows_here = latents.shape[2]
     chans = mid_weight.shape[2]
-    mixed = spans(
+    on_edge = lax.axis_size("row") == 2 and rows_here == 2 and chans == 3 * LANES
+    mixed = (edge_spans if on_edge else spans)(
         latents,
         dispatch_plan,
         span_counts,

time: 24.9 us -> 19.8 us (0.80)
  Pallas kernels: 23.8 us -> 18.7 us
    pallas_call x1, Pallas kernels: 23.8 us -> 18.7 us  [edge_spans(): pl.pallas_call(functools.partial(edge_kernel, req_n), out_shape=jax.Shape...]
where the time goes in v1:
time: 19.8 us; the launch traced here: 19.6 us
  Pallas kernels  18.7 us (94%)
  local copies, waits for them, and re-layouts  0.86 us (4%)
    pallas_call x1, Pallas kernels, edge_spans(): pl.pallas_call(functools.partial(edge_kernel, req_n), out_shape=jax.Shape...  18.7 us
    reshape x1, local copies, waits for them, and re-layouts, local(): return mixed.reshape(1, CF, rows_here, W * chans)  0.86 us

profile of v1, /device:TPU:0, one launch (start us, length us, event | category | flops | bytes accessed | tf_op | source)
XLA Modules:
  0.0 19.6 jit_solution(6494095142142489228)
XLA Ops:
  0.0 18.7 %edge_spans.1 = bf16[2,2,160,384]{3,2,1,0:T(8,128)(2,1)S(1)} custom-call(bf16[8,2,2,320]{3,2,1,0:T(2,128)(2,1)} %lat_hbm.1, s32[8]{0:T(128)} %plan_hbm.1, s32[4]{0:T(128)} %counts_hbm.1, bf16[432,384]{1,0:T(8,128)(2,1)} %in_w_hbm.1, f32[384]{0:T(512)} %in_b_hbm.1, f32[384]{0:T(512)} %gain_hbm.1, f32[384]{0:T(512)} %nbias_hbm.1, ...), custom_call_target="tpu_custom_call" | custom-call | tf_op jit(solution)/shard_map/edge_spans/pallas_call | solution.py:649
  18.8 0.9 %reshape.3 = bf16[1,2,2,61440]{3,2,1,0:T(2,128)(2,1)} reshape(bf16[2,2,160,384]{3,2,1,0:T(8,128)(2,1)S(1)} %edge_spans.1) | data formatting | bytes 983040 | tf_op jit(solution)/shard_map/reshape | solution.py:725

commit v2 on v1

--- a/solution.py
+++ b/solution.py
@@ -13,6 +13,7 @@
 W = 160
 LANES = 128
 DEPTH = 3
+PARTS = ((0, 3),)
 MESH = pl.DeviceIdType.MESH
 
 
@@ -379,8 +380,15 @@
     rows_here = lat_ref.shape[2]
 
     def peer(k):
-        target = lax.rem(flat + k, devices)
+        target = jnp.int32(0)
+        bit = 1
+        while bit < devices:
+            mine = lax.rem(flat // bit, 2)
+            target = target + bit * ((1 - mine) if k & bit else mine)
+            bit *= 2
         return {"row": target // req_n, "req": lax.rem(target, req_n)}
+
+    order = sorted(range(1, devices), key=lambda k: ((k % req_n) * 2 + k // req_n))
 
     def turned(i):
         return jnp.where(me_row == 0, i, 2 - i)
@@ -426,16 +434,22 @@
     for flip in range(2):
         for d in range(DEPTH - 1):
             sel[flip, d] = jnp.zeros_like(sel[flip, d])
+    lanes = lat_ref.shape[3]
+    half = LANES // 2
+    odd = lax.rem(me, 2) == 1
     for d in range(req_n):
         span = lat_ref[plan_ref[d]].astype(jnp.float32)
-        both = jnp.concatenate([span[f] for f in range(CF)], axis=1)
+        late = jnp.concatenate(
+            [span[0, :, half:], span[1, :, :half], span[0, :, :half], span[1, :, half:]], axis=1
+        )
+        soon = jnp.concatenate([span[0], span[1, :, lanes - half :], span[1, :, : lanes - half]], axis=1)
+        both = jnp.where(odd, late, soon)
         sel[0, d + DEPTH - 1] = both.astype(sel.dtype)
         sel[1, d + DEPTH - 1] = jnp.concatenate([both[1:], both[:1]], axis=0).astype(sel.dtype)
     pl.semaphore_wait(barrier, devices - 1)
-    early = DEPTH - 1
-    sends = [[], []]
-    for part, (base, count) in enumerate(((0, early), (early, 1))):
-        for k in range(1, devices):
+    sends = [[] for _ in PARTS]
+    for part, (base, count) in enumerate(PARTS):
+        for k in order:
             where = peer(k)
             there = where["row"]
             send = pltpu.make_async_remote_copy(
@@ -454,7 +468,6 @@
 
     frames_in = DEPTH * CF
     height = row_n * rows_here
-    lanes = x_ref.shape[4] // CF
     width = req_n * lanes // C_LAT
     blocks = width * C_LAT // LANES
     chans = in_w_ref.shape[1]
@@ -520,18 +533,27 @@
             view = jnp.where(mine, after, view)
         return view
 
-    def place_frame(f, slot):
+    left = lax.broadcasted_iota(jnp.int32, (rows_here, LANES), 1) < half
+    reach = -(-blocks // 8) * 8
+
+    def gather(slot, kind):
+        parts = [fan[slot, kind, pl.ds(b, 8, stride=reach), :] for b in range(blocks)]
+        return jnp.concatenate(parts, axis=0)
+
+    def place_frame(f, slot, keep):
         cells = [lines[slot, y // 2, pl.ds(y % 2, blocks, stride=2), :] for y in range(4)]
+        if keep is not None:
+            cells = [cell * keep for cell in cells]
         for p in range(8):
             third = window(cells[2], p, 2 * three)
             inner = jnp.where(lane < 2 * three, window(cells[1], p, three), third)
-            rows = pl.ds(p, blocks, stride=8)
+            rows = slice(p * reach, p * reach + blocks)
             fan[slot, 0, rows, :] = jnp.where(lane < three, window(cells[0], p, 0), inner)
             fan[slot, 1, rows, :] = jnp.where(lane < three, window(cells[3], p, 0), inner)
             fan[slot, 2, rows, :] = third
         for g in range(2):
-            slab[g, f] = fan[slot, g].astype(jnp.bfloat16)
-        last = fan[slot, 2]
+            slab[g, f] = gather(slot, g).astype(jnp.bfloat16)
+        last = gather(slot, 2)
         for t in range(3):
             if 0 <= f - t < outs:
                 at = slice(t * C_LAT, (t + 1) * C_LAT)
@@ -539,23 +561,29 @@
                 tail[f - t, :, at] = moved[:, at].astype(jnp.bfloat16)
 
     def place_span(span, keep):
+        full = lanes // LANES
         for r in range(2):
-            shards = []
-            for q in range(req_n):
-                shard = x_ref[r, q, span].astype(jnp.float32)
-                shards.append(shard if keep is None else shard * keep)
-            for frame in range(CF):
-                merged = jnp.concatenate(
-                    [shard[:, frame * lanes : (frame + 1) * lanes] for shard in shards], axis=1
-                )
-                for b in range(blocks):
-                    lines[frame, r, b * 2 : (b + 1) * 2, :] = merged[:, b * LANES : (b + 1) * LANES]
+            for pair in range(req_n // 2):
+                even = x_ref[r, 2 * pair, span].astype(jnp.float32)
+                late = x_ref[r, 2 * pair + 1, span].astype(jnp.float32)
+                cut = full * LANES
+                mids = [shard[:, cut : cut + LANES] for shard in (even, late)]
+                for frame in range(CF):
+                    start = frame * (cut + LANES)
+                    pieces = [even[:, start + n * LANES : start + (n + 1) * LANES] for n in range(full)]
+                    if frame == 0:
+                        pieces.append(jnp.where(left, mids[0], mids[1]))
+                    else:
+                        pieces.append(pltpu.roll(jnp.where(left, mids[1], mids[0]), half, 1))
+                    pieces += [late[:, start + n * LANES : start + (n + 1) * LANES] for n in range(full)]
+                    for n, piece in enumerate(pieces):
+                        b = pair * (2 * full + 1) + n
+                        lines[frame, r, b * 2 : (b + 1) * 2, :] = piece
         for frame in range(CF):
-            place_frame(span * CF + frame, frame)
-
-    def first_conv(f0):
-        sums = []
-        for g in range(2):
+            place_frame(span * CF + frame, frame, keep)
+
+    def first_dot(f0, g, sums):
+        if True:
             stacked = jnp.concatenate(
                 [slab[g, f0 + t : f0 + t + 2].reshape(2 * width, LANES) for t in range(3)]
                 + [tail[f0 : f0 + 2].reshape(2 * width, LANES)],
@@ -570,6 +598,8 @@
                     pair = (jnp.sum(part, axis=0, keepdims=True), jnp.sum(part * part, axis=0, keepdims=True))
                     total = pair if total is None else (total[0] + pair[0], total[1] + pair[1])
                 sums.append(total)
+
+    def group_stats(f0, sums):
         rows = []
         for f in range(2):
             rows.append(sums[f][0] + sums[2 + f][0])
@@ -583,6 +613,7 @@
             jnp.concatenate([upper, middle, lower], axis=0), same_ref[...], preferred_element_type=jnp.float32
         )
         grouped = (grouped[0:4] + grouped[4:8] + grouped[8:12]) / (height * width * per_group)
+        scaling = []
         for f in range(2):
             mean = grouped[2 * f : 2 * f + 1]
             var = grouped[2 * f + 1 : 2 * f + 2] - mean * mean
@@ -592,48 +623,80 @@
             if f0 + f < CF:
                 half_scale = half_scale * keep_own
                 half_shift = half_shift * keep_own
-            for s in range(3):
-                value = hid[f0 + f, s] * half_scale + half_shift
-                act[f0 + f, s] = (value * (1.0 + jnp.tanh(value))).astype(jnp.bfloat16)
+            scaling.append((half_scale, half_shift))
+        return scaling
+
+    def activate(f, s, half_scale, half_shift):
+        value = hid[f, s] * half_scale + half_shift
+        act[f, s] = (value * (1.0 + jnp.tanh(value))).astype(jnp.bfloat16)
 
     for send in sends[0]:
         send.wait()
+    for copy in copies:
+        copy.wait()
     place_span(0, keep_prev)
     place_span(1, keep_own)
-    first_conv(0)
-    for send in sends[1]:
-        send.wait()
+    early, later = [], []
+    first_dot(0, 0, early)
+    first_dot(0, 1, early)
     place_span(2, None)
-    first_conv(2)
+    scaling = group_stats(0, early)
+    first_dot(2, 0, later)
+    for s in range(3):
+        activate(0, s, *scaling[0])
+    first_dot(2, 1, later)
+    for s in range(3):
+        activate(1, s, *scaling[1])
+    scaling = group_stats(2, later)
+    for f in range(2):
+        for s in range(3):
+            activate(2 + f, s, *scaling[f])
 
     many = CF * width
-    for copy in copies:
-        copy.wait()
-    nil = jnp.zeros((1, 2 * LANES), jnp.float32)
-    for c0, c1 in ((0, 2 * LANES), (2 * LANES, chans)):
-        for o in (1, 0):
-            slabs = []
-            weights = []
-            for t in range(3):
-                for s in range(3):
-                    i = s - o + 1
-                    if 0 <= i < 3 and s - o < 2:
-                        tap = 3 * (3 * t + i)
-                        slabs.append(act[t : t + CF, s].reshape(many, chans))
-                        weights.append(jnp.concatenate([mid_w[tap + j, :, c0:c1] for j in range(3)], axis=1))
-            columns = jnp.dot(
-                jnp.concatenate(slabs, axis=1),
-                jnp.concatenate(weights, axis=0),
-                preferred_element_type=jnp.float32,
-            )
-            size = c1 - c0
-            where = lax.rem(me_row + o, 2)
-            for f in range(CF):
-                part = columns[f * width : (f + 1) * width]
-                total = hid[outs - CF + f, o, :, c0:c1] + mid_b[:, c0:c1] + part[:, size : 2 * size]
-                total = total + jnp.concatenate([nil[:, :size], part[:-1, :size]], axis=0)
-                total = total + jnp.concatenate([part[1:, 2 * size :], nil[:, :size]], axis=0)
-                out_ref[f, where, :, c0:c1] = total.astype(jnp.bfloat16)
+    wide = 2 * LANES
+    nil = jnp.zeros((1, wide), jnp.float32)
+
+    def second_dot(picks, cells):
+        slabs = []
+        weights = []
+        for t in range(3):
+            for s in cells:
+                row = picks(3 * t, s)
+                slabs.append(act[t : t + CF, s].reshape(many, chans))
+                weights.append(jnp.concatenate(row, axis=1))
+        return jnp.dot(
+            jnp.concatenate(slabs, axis=1), jnp.concatenate(weights, axis=0), preferred_element_type=jnp.float32
+        )
+
+    def finish(o, c0, c1, before, here, after):
+        size = c1 - c0
+        where = lax.rem(me_row + o, 2)
+        for f in range(CF):
+            rows = slice(f * width, (f + 1) * width)
+            total = hid[outs - CF + f, o, :, c0:c1] + mid_b[:, c0:c1] + here[rows]
+            total = total + jnp.concatenate([nil[:, :size], before[rows][:-1]], axis=0)
+            total = total + jnp.concatenate([after[rows][1:], nil[:, :size]], axis=0)
+            out_ref[f, where, :, c0:c1] = total.astype(jnp.bfloat16)
+
+    for o in (1, 0):
+        columns = second_dot(
+            lambda t, s: [mid_w[3 * (t + s - o + 1) + j, :, :wide] for j in range(3)], range(2 + o)
+        )
+        finish(o, 0, wide, *(columns[:, j * wide : (j + 1) * wide] for j in range(3)))
+    void = jnp.zeros((chans, LANES), jnp.bfloat16)
+    ends = second_dot(
+        lambda t, s: [
+            mid_w[3 * (t + s - o + 1) + 2, :, wide:] if s - o < 2 else void for o in range(2)
+        ],
+        range(3),
+    )
+    for o in (1, 0):
+        columns = second_dot(
+            lambda t, s: [mid_w[3 * (t + s - o + 1) + j, :, wide:] for j in range(2)], range(2 + o)
+        )
+        finish(
+            o, wide, chans, columns[:, :LANES], columns[:, LANES:], ends[:, o * LANES : (o + 1) * LANES]
+        )
 
 
 def edge_spans(latents, dispatch_plan, span_counts, in_weight, in_bias, norm_gain, norm_bias, mid_weight, mid_bias):
@@ -670,10 +733,10 @@
             pltpu.VMEM((outs, height, width, chans), jnp.float32),
             pltpu.VMEM((outs, rows_here + 1, width, chans), jnp.bfloat16),
             pltpu.VMEM((CF, 2, 2 * blocks, LANES), jnp.float32),
-            pltpu.VMEM((CF, 3, width, LANES), jnp.float32),
+            pltpu.VMEM((CF, 3, 8 * (-(-blocks // 8) * 8), LANES), jnp.float32),
             pltpu.SemaphoreType.DMA((25,)),
-            pltpu.SemaphoreType.DMA((2, req_n * row_n)),
-            pltpu.SemaphoreType.DMA((2, req_n * row_n)),
+            pltpu.SemaphoreType.DMA((len(PARTS), req_n * row_n)),
+            pltpu.SemaphoreType.DMA((len(PARTS), req_n * row_n)),
         ],
         compiler_params=pltpu.CompilerParams(
             collective_id=0, has_side_effects=True, vmem_limit_bytes=48 << 20
@@ -710,7 +773,9 @@
 ):
     rows_here = latents.shape[2]
     chans = mid_weight.shape[2]
-    on_edge = lax.axis_size("row") == 2 and rows_here == 2 and chans == 3 * LANES
+    req_n = lax.axis_size("req")
+    halves = latents.shape[3] % LANES == LANES // 2 and req_n & (req_n - 1) == 0
+    on_edge = halves and lax.axis_size("row") == 2 and rows_here == 2 and chans == 3 * LANES
     mixed = (edge_spans if on_edge else spans)(
         latents,
         dispatch_plan,

time: 19.8 us -> 18.7 us (0.944)
  Pallas kernels: 18.7 us -> 17.7 us
    pallas_call x1, Pallas kernels: 18.7 us -> 17.7 us  [edge_spans(): pl.pallas_call(functools.partial(edge_kernel, req_n), out_shape=jax.Shape...]
where the time goes in v2:
time: 18.7 us; the launch traced here: 18.6 us
  Pallas kernels  17.7 us (95%)
  local copies, waits for them, and re-layouts  0.86 us (5%)
    pallas_call x1, Pallas kernels, edge_spans(): pl.pallas_call(functools.partial(edge_kernel, req_n), out_shape=jax.Shape...  17.7 us
    reshape x1, local copies, waits for them, and re-layouts, local(): return mixed.reshape(1, CF, rows_here, W * chans)  0.86 us

profile of v2, /device:TPU:0, one launch (start us, length us, event | category | flops | bytes accessed | tf_op | source)
XLA Modules:
  0.0 18.6 jit_solution(9089336382528868720)
XLA Ops:
  0.0 17.7 %edge_spans.1 = bf16[2,2,160,384]{3,2,1,0:T(8,128)(2,1)S(1)} custom-call(bf16[8,2,2,320]{3,2,1,0:T(2,128)(2,1)} %lat_hbm.1, s32[8]{0:T(128)} %plan_hbm.1, s32[4]{0:T(128)} %counts_hbm.1, bf16[432,384]{1,0:T(8,128)(2,1)} %in_w_hbm.1, f32[384]{0:T(512)} %in_b_hbm.1, f32[384]{0:T(512)} %gain_hbm.1, f32[384]{0:T(512)} %nbias_hbm.1, ...), custom_call_target="tpu_custom_call" | custom-call | tf_op jit(solution)/shard_map/edge_spans/pallas_call | solution.py:712
  17.7 0.9 %reshape.3 = bf16[1,2,2,61440]{3,2,1,0:T(2,128)(2,1)} reshape(bf16[2,2,160,384]{3,2,1,0:T(8,128)(2,1)S(1)} %edge_spans.1) | data formatting | bytes 983040 | tf_op jit(solution)/shard_map/reshape | solution.py:790

commit v3 on v2

--- a/solution.py
+++ b/solution.py
@@ -13,7 +13,6 @@
 W = 160
 LANES = 128
 DEPTH = 3
-PARTS = ((0, 3),)
 MESH = pl.DeviceIdType.MESH
 
 
@@ -376,26 +375,19 @@
     me_row = lax.axis_index("row")
     row_n = 2
     devices = req_n * row_n
-    flat = me_row * req_n + me
+    rank = me // 2 * 4 + me_row * 2 + lax.rem(me, 2)
     rows_here = lat_ref.shape[2]
 
-    def peer(k):
-        target = jnp.int32(0)
-        bit = 1
-        while bit < devices:
-            mine = lax.rem(flat // bit, 2)
-            target = target + bit * ((1 - mine) if k & bit else mine)
-            bit *= 2
-        return {"row": target // req_n, "req": lax.rem(target, req_n)}
-
-    order = sorted(range(1, devices), key=lambda k: ((k % req_n) * 2 + k // req_n))
+    def peer(n):
+        other = n + jnp.where(n >= rank, 1, 0)
+        return other, {"row": lax.rem(other // 2, 2), "req": other // 4 * 2 + lax.rem(other, 2)}
 
     def turned(i):
         return jnp.where(me_row == 0, i, 2 - i)
 
     barrier = pltpu.get_barrier_semaphore()
-    for k in range(1, devices):
-        pl.semaphore_signal(barrier, inc=1, device_id=peer(k), device_id_type=MESH)
+    for n in range(devices - 1):
+        pl.semaphore_signal(barrier, inc=1, device_id=peer(n)[1], device_id_type=MESH)
     loads = [
         pltpu.make_async_copy(source, target, sems.at[n])
         for n, (source, target) in enumerate(
@@ -447,21 +439,26 @@
         sel[0, d + DEPTH - 1] = both.astype(sel.dtype)
         sel[1, d + DEPTH - 1] = jnp.concatenate([both[1:], both[:1]], axis=0).astype(sel.dtype)
     pl.semaphore_wait(barrier, devices - 1)
-    sends = [[] for _ in PARTS]
-    for part, (base, count) in enumerate(PARTS):
-        for k in order:
-            where = peer(k)
-            there = where["row"]
-            send = pltpu.make_async_remote_copy(
-                src_ref=sel.at[there, pl.ds(where["req"] + base, count)],
-                dst_ref=x_ref.at[lax.rem(me_row + there, 2), me, pl.ds(base, count)],
-                send_sem=send_sems.at[part, k],
-                recv_sem=recv_sems.at[part, k],
+    sends = []
+    arrivals = []
+    for n in range(devices - 1):
+        other, where = peer(n)
+        there = where["row"]
+
+        def copy_with(received):
+            return pltpu.make_async_remote_copy(
+                src_ref=sel.at[there, pl.ds(where["req"], DEPTH)],
+                dst_ref=x_ref.at[lax.rem(me_row + there, 2), me],
+                send_sem=send_sems.at[n],
+                recv_sem=recv_sems.at[received],
                 device_id=where,
                 device_id_type=MESH,
             )
-            send.start()
-            sends[part].append(send)
+
+        send = copy_with(rank)
+        send.start()
+        sends.append(send)
+        arrivals.append(copy_with(other))
     x_ref[0, me] = sel[me_row, pl.ds(me, DEPTH)]
     for copy in loads[2:] + in_copies:
         copy.wait()
@@ -630,8 +627,10 @@
         value = hid[f, s] * half_scale + half_shift
         act[f, s] = (value * (1.0 + jnp.tanh(value))).astype(jnp.bfloat16)
 
-    for send in sends[0]:
-        send.wait()
+    for send in sends:
+        send.wait_send()
+    for arrival in arrivals:
+        arrival.wait_recv()
     for copy in copies:
         copy.wait()
     place_span(0, keep_prev)
@@ -735,8 +734,8 @@
             pltpu.VMEM((CF, 2, 2 * blocks, LANES), jnp.float32),
             pltpu.VMEM((CF, 3, 8 * (-(-blocks // 8) * 8), LANES), jnp.float32),
             pltpu.SemaphoreType.DMA((25,)),
-            pltpu.SemaphoreType.DMA((len(PARTS), req_n * row_n)),
-            pltpu.SemaphoreType.DMA((len(PARTS), req_n * row_n)),
+            pltpu.SemaphoreType.DMA((req_n * row_n,)),
+            pltpu.SemaphoreType.DMA((req_n * row_n,)),
         ],
         compiler_params=pltpu.CompilerParams(
             collective_id=0, has_side_effects=True, vmem_limit_bytes=48 << 20

time: 18.7 us -> 17.9 us (0.957)
  Pallas kernels: 17.7 us -> 16.9 us
    pallas_call x1, Pallas kernels: 17.7 us -> 16.9 us  [edge_spans(): pl.pallas_call(functools.partial(edge_kernel, req_n), out_shape=jax.Shape...]
where the time goes in v3:
time: 17.9 us; the launch traced here: 17.8 us
  Pallas kernels  16.9 us (94%)
  local copies, waits for them, and re-layouts  0.86 us (5%)
    pallas_call x1, Pallas kernels, edge_spans(): pl.pallas_call(functools.partial(edge_kernel, req_n), out_shape=jax.Shape...  16.9 us
    reshape x1, local copies, waits for them, and re-layouts, local(): return mixed.reshape(1, CF, rows_here, W * chans)  0.86 us

profile of v3, /device:TPU:0, one launch (start us, length us, event | category | flops | bytes accessed | tf_op | source)
XLA Modules:
  0.0 17.8 jit_solution(16409787722729672026)
XLA Ops:
  0.0 16.9 %edge_spans.1 = bf16[2,2,160,384]{3,2,1,0:T(8,128)(2,1)S(1)} custom-call(bf16[8,2,2,320]{3,2,1,0:T(2,128)(2,1)} %lat_hbm.1, s32[8]{0:T(128)} %plan_hbm.1, s32[4]{0:T(128)} %counts_hbm.1, bf16[432,384]{1,0:T(8,128)(2,1)} %in_w_hbm.1, f32[384]{0:T(512)} %in_b_hbm.1, f32[384]{0:T(512)} %gain_hbm.1, f32[384]{0:T(512)} %nbias_hbm.1, ...), custom_call_target="tpu_custom_call" | custom-call | tf_op jit(solution)/shard_map/edge_spans/pallas_call | solution.py:711
  16.9 0.9 %reshape.3 = bf16[1,2,2,61440]{3,2,1,0:T(2,128)(2,1)} reshape(bf16[2,2,160,384]{3,2,1,0:T(8,128)(2,1)S(1)} %edge_spans.1) | data formatting | bytes 983040 | tf_op jit(solution)/shard_map/reshape | solution.py:789

commit v4 on v3

--- a/solution.py
+++ b/solution.py
@@ -506,9 +506,22 @@
                 else:
                     tap = (3 * t + i) * three + two
                     in_w[g, base : base + C_LAT, columns] = in_w_ref[tap : tap + C_LAT, :]
-        in_w[g, 3 * LANES + three :, :] = jnp.zeros((LANES - three, 2 * chans), jnp.bfloat16)
+        in_w[g, 3 * LANES + three : 4 * LANES - C_LAT, :] = jnp.zeros(
+            (LANES - three - C_LAT, 2 * chans), jnp.bfloat16
+        )
+    place = lax.broadcasted_iota(jnp.int32, (C_LAT, chans), 0)
+    left_over = jnp.broadcast_to(in_b, (C_LAT, chans))
+    bias_rows = jnp.zeros((C_LAT, chans), jnp.float32)
+    for n in range(3):
+        digits = left_over.astype(jnp.bfloat16).astype(jnp.float32)
+        bias_rows = jnp.where(place == n, digits, bias_rows)
+        left_over = left_over - digits
+    for g in range(2):
+        for o in range(2):
+            in_w[g, 4 * LANES - C_LAT :, o * chans : (o + 1) * chans] = bias_rows.astype(jnp.bfloat16)
+    ones = jnp.where(lax.broadcasted_iota(jnp.int32, (width, LANES), 1) >= LANES - C_LAT, 1.0, 0.0)
     for f in range(outs):
-        tail[f] = jnp.zeros((width, LANES), jnp.bfloat16)
+        tail[f] = ones.astype(jnp.bfloat16)
     per_group = chans // G
     down = lax.broadcasted_iota(jnp.int32, (chans, chans), 0) // per_group
     over = lax.broadcasted_iota(jnp.int32, (chans, chans), 1) // per_group
@@ -590,7 +603,7 @@
             for f in range(2):
                 total = None
                 for o in range(2):
-                    part = both[f * width : (f + 1) * width, o * chans : (o + 1) * chans] + in_b
+                    part = both[f * width : (f + 1) * width, o * chans : (o + 1) * chans]
                     hid[f0 + f, 2 * g + o] = part
                     pair = (jnp.sum(part, axis=0, keepdims=True), jnp.sum(part * part, axis=0, keepdims=True))
                     total = pair if total is None else (total[0] + pair[0], total[1] + pair[1])
@@ -635,21 +648,22 @@
         copy.wait()
     place_span(0, keep_prev)
     place_span(1, keep_own)
+    place_span(2, None)
     early, later = [], []
     first_dot(0, 0, early)
     first_dot(0, 1, early)
-    place_span(2, None)
+    first_dot(2, 0, later)
     scaling = group_stats(0, early)
-    first_dot(2, 0, later)
+    first_dot(2, 1, later)
     for s in range(3):
         activate(0, s, *scaling[0])
-    first_dot(2, 1, later)
     for s in range(3):
         activate(1, s, *scaling[1])
     scaling = group_stats(2, later)
-    for f in range(2):
-        for s in range(3):
-            activate(2 + f, s, *scaling[f])
+    for s in range(3):
+        activate(2, s, *scaling[0])
+    for s in range(3):
+        activate(3, s, *scaling[1])
 
     many = CF * width
     wide = 2 * LANES

time: 17.9 us -> 17.5 us (0.978)
  Pallas kernels: 16.9 us -> 16.4 us
    pallas_call x1, Pallas kernels: 16.9 us -> 16.4 us  [edge_spans(): pl.pallas_call(functools.partial(edge_kernel, req_n), out_shape=jax.Shape...]
where the time goes in v4:
time: 17.5 us; the launch traced here: 17.3 us
  Pallas kernels  16.4 us (94%)
  local copies, waits for them, and re-layouts  0.86 us (5%)
    pallas_call x1, Pallas kernels, edge_spans(): pl.pallas_call(functools.partial(edge_kernel, req_n), out_shape=jax.Shape...  16.4 us
    reshape x1, local copies, waits for them, and re-layouts, local(): return mixed.reshape(1, CF, rows_here, W * chans)  0.86 us

profile of v4, /device:TPU:0, one launch (start us, length us, event | category | flops | bytes accessed | tf_op | source)
XLA Modules:
  0.0 17.3 jit_solution(14911207356921374759)
XLA Ops:
  0.0 16.4 %edge_spans.1 = bf16[2,2,160,384]{3,2,1,0:T(8,128)(2,1)S(1)} custom-call(bf16[8,2,2,320]{3,2,1,0:T(2,128)(2,1)} %lat_hbm.1, s32[8]{0:T(128)} %plan_hbm.1, s32[4]{0:T(128)} %counts_hbm.1, bf16[432,384]{1,0:T(8,128)(2,1)} %in_w_hbm.1, f32[384]{0:T(512)} %in_b_hbm.1, f32[384]{0:T(512)} %gain_hbm.1, f32[384]{0:T(512)} %nbias_hbm.1, ...), custom_call_target="tpu_custom_call" | custom-call | tf_op jit(solution)/shard_map/edge_spans/pallas_call | solution.py:725
  16.5 0.9 %reshape.3 = bf16[1,2,2,61440]{3,2,1,0:T(2,128)(2,1)} reshape(bf16[2,2,160,384]{3,2,1,0:T(8,128)(2,1)S(1)} %edge_spans.1) | data formatting | bytes 983040 | tf_op jit(solution)/shard_map/reshape | solution.py:803

commit v5 on v4

--- a/solution.py
+++ b/solution.py
@@ -439,26 +439,36 @@
         sel[0, d + DEPTH - 1] = both.astype(sel.dtype)
         sel[1, d + DEPTH - 1] = jnp.concatenate([both[1:], both[:1]], axis=0).astype(sel.dtype)
     pl.semaphore_wait(barrier, devices - 1)
-    sends = []
-    arrivals = []
-    for n in range(devices - 1):
-        other, where = peer(n)
-        there = where["row"]
-
-        def copy_with(received):
-            return pltpu.make_async_remote_copy(
-                src_ref=sel.at[there, pl.ds(where["req"], DEPTH)],
-                dst_ref=x_ref.at[lax.rem(me_row + there, 2), me],
-                send_sem=send_sems.at[n],
-                recv_sem=recv_sems.at[received],
-                device_id=where,
-                device_id_type=MESH,
-            )
-
-        send = copy_with(rank)
-        send.start()
-        sends.append(send)
-        arrivals.append(copy_with(other))
+    def spans_of(req):
+        count = min(DEPTH, req + 1)
+        return DEPTH - count, count
+
+    def copy_to(n, received):
+        row, req = n // 2 % 2, n // 4 * 2 + n % 2
+        base, count = spans_of(req)
+        return pltpu.make_async_remote_copy(
+            src_ref=sel.at[row, pl.ds(req + base, count)],
+            dst_ref=x_ref.at[lax.rem(me_row + row, 2), me, pl.ds(base, count)],
+            send_sem=send_sems.at[n],
+            recv_sem=recv_sems.at[received],
+            device_id={"row": jnp.int32(row), "req": jnp.int32(req)},
+            device_id_type=MESH,
+        )
+
+    for n in range(devices):
+
+        @pl.when(rank != n)
+        def _(n=n):
+            copy_to(n, rank).start()
+
+    for req in range(DEPTH - 1):
+
+        @pl.when(me == req)
+        def _(base=spans_of(req)[0]):
+            for r in range(2):
+                for q in range(req_n):
+                    x_ref[r, q, :base] = jnp.zeros_like(x_ref[r, q, :base])
+
     x_ref[0, me] = sel[me_row, pl.ds(me, DEPTH)]
     for copy in loads[2:] + in_copies:
         copy.wait()
@@ -527,7 +537,9 @@
     over = lax.broadcasted_iota(jnp.int32, (chans, chans), 1) // per_group
     same_ref[...] = jnp.where(down == over, 1.0, 0.0).astype(jnp.bfloat16)
 
-    lane = lax.broadcasted_iota(jnp.int32, (blocks, LANES), 1)
+    group = CF * blocks
+    lane = lax.broadcasted_iota(jnp.int32, (group, LANES), 1)
+    line = lax.rem(lax.broadcasted_iota(jnp.int32, (group, LANES), 0), blocks)
     nothing = jnp.zeros((1, LANES), jnp.float32)
 
     def window(cells, p, place):
@@ -535,40 +547,42 @@
         if p == 0:
             before = jnp.concatenate([nothing, view[:-1]], axis=0)
             mine = jnp.logical_and(lane >= place, lane < place + C_LAT)
-            view = jnp.where(mine, before, view)
+            view = jnp.where(mine, jnp.where(line == 0, 0.0, before), view)
         if p == 7:
             after = jnp.concatenate([view[1:], nothing], axis=0)
             edge = (place + two) % LANES
             mine = jnp.logical_and(lane >= edge, lane < edge + C_LAT)
-            view = jnp.where(mine, after, view)
+            view = jnp.where(mine, jnp.where(line == blocks - 1, 0.0, after), view)
         return view
 
     left = lax.broadcasted_iota(jnp.int32, (rows_here, LANES), 1) < half
-    reach = -(-blocks // 8) * 8
-
-    def gather(slot, kind):
-        parts = [fan[slot, kind, pl.ds(b, 8, stride=reach), :] for b in range(blocks)]
+    reach = -(-group // 8) * 8
+
+    def gather(span, frame, kind):
+        parts = [fan[span, kind, pl.ds(frame * blocks + b, 8, stride=reach), :] for b in range(blocks)]
         return jnp.concatenate(parts, axis=0)
 
-    def place_frame(f, slot, keep):
-        cells = [lines[slot, y // 2, pl.ds(y % 2, blocks, stride=2), :] for y in range(4)]
+    def place_frames(span, keep):
+        cells = [lines[span, y // 2, pl.ds(y % 2, group, stride=2), :] for y in range(4)]
         if keep is not None:
             cells = [cell * keep for cell in cells]
         for p in range(8):
             third = window(cells[2], p, 2 * three)
             inner = jnp.where(lane < 2 * three, window(cells[1], p, three), third)
-            rows = slice(p * reach, p * reach + blocks)
-            fan[slot, 0, rows, :] = jnp.where(lane < three, window(cells[0], p, 0), inner)
-            fan[slot, 1, rows, :] = jnp.where(lane < three, window(cells[3], p, 0), inner)
-            fan[slot, 2, rows, :] = third
-        for g in range(2):
-            slab[g, f] = gather(slot, g).astype(jnp.bfloat16)
-        last = gather(slot, 2)
-        for t in range(3):
-            if 0 <= f - t < outs:
-                at = slice(t * C_LAT, (t + 1) * C_LAT)
-                moved = pltpu.roll(last, t * C_LAT, 1) if t else last
-                tail[f - t, :, at] = moved[:, at].astype(jnp.bfloat16)
+            rows = slice(p * reach, p * reach + group)
+            fan[span, 0, rows, :] = jnp.where(lane < three, window(cells[0], p, 0), inner)
+            fan[span, 1, rows, :] = jnp.where(lane < three, window(cells[3], p, 0), inner)
+            fan[span, 2, rows, :] = third
+        for frame in range(CF):
+            f = span * CF + frame
+            for g in range(2):
+                slab[g, f] = gather(span, frame, g).astype(jnp.bfloat16)
+            last = gather(span, frame, 2)
+            for t in range(3):
+                if 0 <= f - t < outs:
+                    at = slice(t * C_LAT, (t + 1) * C_LAT)
+                    moved = pltpu.roll(last, t * C_LAT, 1) if t else last
+                    tail[f - t, :, at] = moved[:, at].astype(jnp.bfloat16)
 
     def place_span(span, keep):
         full = lanes // LANES
@@ -588,9 +602,9 @@
                     pieces += [late[:, start + n * LANES : start + (n + 1) * LANES] for n in range(full)]
                     for n, piece in enumerate(pieces):
                         b = pair * (2 * full + 1) + n
-                        lines[frame, r, b * 2 : (b + 1) * 2, :] = piece
-        for frame in range(CF):
-            place_frame(span * CF + frame, frame, keep)
+                        row = 2 * (frame * blocks + b)
+                        lines[span, r, row : row + 2, :] = piece
+        place_frames(span, keep)
 
     def first_dot(f0, g, sums):
         if True:
@@ -640,10 +654,27 @@
         value = hid[f, s] * half_scale + half_shift
         act[f, s] = (value * (1.0 + jnp.tanh(value))).astype(jnp.bfloat16)
 
-    for send in sends:
-        send.wait_send()
-    for arrival in arrivals:
-        arrival.wait_recv()
+    for n in range(devices):
+
+        @pl.when(rank != n)
+        def _(n=n):
+            copy_to(n, rank).wait_send()
+
+    for req in range(DEPTH):
+
+        @pl.when(me == req if req < DEPTH - 1 else me >= req)
+        def _(base=spans_of(req)[0], count=spans_of(req)[1]):
+            for n in range(devices - 1):
+                other, where = peer(n)
+                pltpu.make_async_remote_copy(
+                    src_ref=sel.at[0, pl.ds(base, count)],
+                    dst_ref=x_ref.at[0, 0, pl.ds(base, count)],
+                    send_sem=send_sems.at[0],
+                    recv_sem=recv_sems.at[other],
+                    device_id=where,
+                    device_id_type=MESH,
+                ).wait_recv()
+
     for copy in copies:
         copy.wait()
     place_span(0, keep_prev)
@@ -745,8 +776,8 @@
             pltpu.VMEM((outs, width, LANES), jnp.bfloat16),
             pltpu.VMEM((outs, height, width, chans), jnp.float32),
             pltpu.VMEM((outs, rows_here + 1, width, chans), jnp.bfloat16),
-            pltpu.VMEM((CF, 2, 2 * blocks, LANES), jnp.float32),
-            pltpu.VMEM((CF, 3, 8 * (-(-blocks // 8) * 8), LANES), jnp.float32),
+            pltpu.VMEM((DEPTH, 2, 2 * CF * blocks, LANES), jnp.float32),
+            pltpu.VMEM((DEPTH, 3, 8 * (-(-CF * blocks // 8) * 8), LANES), jnp.float32),
             pltpu.SemaphoreType.DMA((25,)),
             pltpu.SemaphoreType.DMA((req_n * row_n,)),
             pltpu.SemaphoreType.DMA((req_n * row_n,)),

time: 17.5 us -> 17.1 us (0.977)
  Pallas kernels: 16.4 us -> 16.1 us
    pallas_call x1, Pallas kernels: 16.4 us -> 16.1 us  [edge_spans(): pl.pallas_call(functools.partial(edge_kernel, req_n), out_shape=jax.Shape...]
where the time goes in v5:
time: 17.1 us; the launch traced here: 17 us
  Pallas kernels  16.1 us (94%)
  local copies, waits for them, and re-layouts  0.86 us (5%)
    pallas_call x1, Pallas kernels, edge_spans(): pl.pallas_call(functools.partial(edge_kernel, req_n), out_shape=jax.Shape...  16.1 us
    reshape x1, local copies, waits for them, and re-layouts, local(): return mixed.reshape(1, CF, rows_here, W * chans)  0.86 us

profile of v5, /device:TPU:0, one launch (start us, length us, event | category | flops | bytes accessed | tf_op | source)
XLA Modules:
  0.0 17.0 jit_solution(6613233104525873261)
XLA Ops:
  0.0 16.1 %edge_spans.1 = bf16[2,2,160,384]{3,2,1,0:T(8,128)(2,1)S(1)} custom-call(bf16[8,2,2,320]{3,2,1,0:T(2,128)(2,1)} %lat_hbm.1, s32[8]{0:T(128)} %plan_hbm.1, s32[4]{0:T(128)} %counts_hbm.1, bf16[432,384]{1,0:T(8,128)(2,1)} %in_w_hbm.1, f32[384]{0:T(512)} %in_b_hbm.1, f32[384]{0:T(512)} %gain_hbm.1, f32[384]{0:T(512)} %nbias_hbm.1, ...), custom_call_target="tpu_custom_call" | custom-call | tf_op jit(solution)/shard_map/edge_spans/pallas_call | solution.py:756
  16.1 0.9 %reshape.3 = bf16[1,2,2,61440]{3,2,1,0:T(2,128)(2,1)} reshape(bf16[2,2,160,384]{3,2,1,0:T(8,128)(2,1)S(1)} %edge_spans.1) | data formatting | bytes 983040 | tf_op jit(solution)/shard_map/reshape | solution.py:834

commit v6 on v5

--- a/solution.py
+++ b/solution.py
@@ -386,7 +386,7 @@
         return jnp.where(me_row == 0, i, 2 - i)
 
     barrier = pltpu.get_barrier_semaphore()
-    for n in range(devices - 1):
+    for n in reversed(range(devices - 1)):
         pl.semaphore_signal(barrier, inc=1, device_id=peer(n)[1], device_id_type=MESH)
     loads = [
         pltpu.make_async_copy(source, target, sems.at[n])
@@ -654,12 +654,6 @@
         value = hid[f, s] * half_scale + half_shift
         act[f, s] = (value * (1.0 + jnp.tanh(value))).astype(jnp.bfloat16)
 
-    for n in range(devices):
-
-        @pl.when(rank != n)
-        def _(n=n):
-            copy_to(n, rank).wait_send()
-
     for req in range(DEPTH):
 
         @pl.when(me == req if req < DEPTH - 1 else me >= req)
@@ -741,6 +735,12 @@
         finish(
             o, wide, chans, columns[:, :LANES], columns[:, LANES:], ends[:, o * LANES : (o + 1) * LANES]
         )
+
+    for n in range(devices):
+
+        @pl.when(rank != n)
+        def _(n=n):
+            copy_to(n, rank).wait_send()
 
 
 def edge_spans(latents, dispatch_plan, span_counts, in_weight, in_bias, norm_gain, norm_bias, mid_weight, mid_bias):

time: 17.1 us -> 17.1 us (level)
  no operation moved by 1% of the time
where the time goes in v6:
time: 17.1 us; the launch traced here: 17 us
  Pallas kernels  16.1 us (94%)
  local copies, waits for them, and re-layouts  0.86 us (5%)
    pallas_call x1, Pallas kernels, edge_spans(): pl.pallas_call(functools.partial(edge_kernel, req_n), out_shape=jax.Shape...  16.1 us
    reshape x1, local copies, waits for them, and re-layouts, local(): return mixed.reshape(1, CF, rows_here, W * chans)  0.86 us

profile of v6, /device:TPU:0, one launch (start us, length us, event | category | flops | bytes accessed | tf_op | source)
XLA Modules:
  0.0 17.0 jit_solution(12370617644188808289)
XLA Ops:
  0.0 16.1 %edge_spans.1 = bf16[2,2,160,384]{3,2,1,0:T(8,128)(2,1)S(1)} custom-call(bf16[8,2,2,320]{3,2,1,0:T(2,128)(2,1)} %lat_hbm.1, s32[8]{0:T(128)} %plan_hbm.1, s32[4]{0:T(128)} %counts_hbm.1, bf16[432,384]{1,0:T(8,128)(2,1)} %in_w_hbm.1, f32[384]{0:T(512)} %in_b_hbm.1, f32[384]{0:T(512)} %gain_hbm.1, f32[384]{0:T(512)} %nbias_hbm.1, ...), custom_call_target="tpu_custom_call" | custom-call | tf_op jit(solution)/shard_map/edge_spans/pallas_call | solution.py:756
  16.1 0.9 %reshape.3 = bf16[1,2,2,61440]{3,2,1,0:T(2,128)(2,1)} reshape(bf16[2,2,160,384]{3,2,1,0:T(8,128)(2,1)S(1)} %edge_spans.1) | data formatting | bytes 983040 | tf_op jit(solution)/shard_map/reshape | solution.py:834
